TPU v7x, 32 devices: a whole 2x2x4 slice. The times are simulated.
32 devices in a mesh: seq: 4 (over y, x), fsdp: 8 (over z, core).
Axes of the slice: x: 2, y: 2, z: 4, core: 2. Of those that a mesh axis runs over, the one named last changes fastest.
Arguments:
- frames: bfloat16 [8, 2048, 1536], P('fsdp', 'seq'), may hold values from -6 to 6
- lengths: int32 [8], P('fsdp'), may hold values from 512 to 2048, as said below
- gain: float32 [1536], replicated, may hold values from 0.5 to 1.5
- w_pointwise: bfloat16 [1536, 3072], P('fsdp'), may hold values from -0.15625 to 0.15625
- w_depthwise: float32 [31, 1536], replicated, may hold values from -1 to 1
- w_output: bfloat16 [1536, 1536], P('fsdp'), may hold values from -0.15625 to 0.15625
- cotangent: bfloat16 [8, 2048, 1536], P('fsdp', 'seq'), may hold values from -6 to 6
Outputs:
- output: bfloat16 [8, 2048, 1536], P('fsdp', 'seq')
- grad_frames: bfloat16 [8, 2048, 1536], P('fsdp', 'seq')
- grad_pointwise: float32 [1536, 3072], P('fsdp')
- grad_output: float32 [1536, 1536], P('fsdp')
- grad_gain: float32 [1536], replicated
- grad_depthwise: float32 [31, 1536], replicated
Inputs may be any that keep to these rules, and one draw needn't show every extreme that they name: `lengths`: the first utterance fills all 2048 slots.
All inputs are finite; a program needn't handle non-finite values.
Results may differ from a plain program's by a relative error of at most 0.014.
Values may be sent and summed in bfloat16 or wider, within the bound.
No kernel may reach another device: no remote copies, remote signals or barrier semaphores. Data moves between devices by JAX's collectives and lax.ppermute only.
A program may use at most 128 MiB of HBM per device.

v0:
```python
import jax
import jax.numpy as jnp
from jax import lax
from jax.sharding import PartitionSpec as P

EPS = 1e-05


def extended(block, sides, width):
    for axis, dim in sides:
        count = lax.axis_size(axis)
        forward = [(i, i + 1) for i in range(count - 1)]
        backward = [(target, source) for source, target in forward]
        low = lax.ppermute(
            lax.slice_in_dim(block, block.shape[dim] - width, None, axis=dim), axis, forward
        )
        high = lax.ppermute(lax.slice_in_dim(block, 0, width, axis=dim), axis, backward)
        block = jnp.concatenate([low, block, high], axis=dim)
    return block


def rounded_term(left, right):
    term = lax.dot_general(
        left, right, (((0,), (0,)), ((), ())), preferred_element_type=jnp.float32
    )
    term = lax.optimization_barrier(term.astype(jnp.bfloat16))
    return term.astype(jnp.float32)


def on_device(frames, lengths, gain, w_pointwise, w_depthwise, w_output, cotangent):
    frame_count = frames.shape[1]
    width = frames.shape[2]
    taps = w_depthwise.shape[0]
    half_width = (taps - 1) // 2
    full_pointwise, full_output = (
        lax.all_gather(w_pointwise, "fsdp", axis=0, tiled=True),
        lax.all_gather(w_output, "fsdp", axis=0, tiled=True),
    )
    as_float = frames[0].astype(jnp.float32)
    center = jnp.mean(as_float, axis=-1, keepdims=True)
    spread = jnp.mean((as_float - center) ** 2, axis=-1, keepdims=True)
    inverse = lax.rsqrt(spread + EPS)
    normed = (as_float - center) * inverse
    lifted = (normed * gain).astype(jnp.bfloat16)
    position = lax.axis_index("seq") * frame_count + jnp.arange(frame_count, dtype=jnp.int32)
    mask = (position < lengths[0]).astype(jnp.float32)[:, None]
    joined = jnp.dot(lifted, full_pointwise, preferred_element_type=jnp.float32)
    value = joined[:, :width]
    gate_sig = jax.nn.sigmoid(joined[:, width:])
    glu = (value * gate_sig * mask).astype(jnp.bfloat16)
    glu_ext = extended(glu[None], (("seq", 1),), half_width)[0].astype(jnp.float32)
    conv = jnp.zeros((frame_count, width), jnp.float32)
    for offset in range(taps):
        conv = conv + w_depthwise[offset] * glu_ext[offset : offset + frame_count]
    conv_sig = jax.nn.sigmoid(conv)
    swished = (conv * conv_sig).astype(jnp.bfloat16)
    branch = jnp.dot(swished, full_output, preferred_element_type=jnp.float32)
    output = (as_float + branch).astype(jnp.bfloat16)
    branch_grad = (cotangent[0].astype(jnp.float32) * mask).astype(jnp.bfloat16)
    swish_grad = lax.dot_general(
        branch_grad, full_output, (((1,), (1,)), ((), ())), preferred_element_type=jnp.float32
    )
    conv_grad = (swish_grad * conv_sig * (1.0 + conv * (1.0 - conv_sig))).astype(jnp.bfloat16)
    grad_ext = extended(conv_grad[None], (("seq", 1),), half_width)[0].astype(jnp.float32)
    conv_grad_f = conv_grad.astype(jnp.float32)
    glu_grad = jnp.zeros((frame_count, width), jnp.float32)
    tap_rows = []
    for offset in range(taps):
        back = taps - 1 - offset
        glu_grad = glu_grad + w_depthwise[offset] * grad_ext[back : back + frame_count]
        tap_rows.append(jnp.sum(conv_grad_f * glu_ext[offset : offset + frame_count], axis=0))
    glu_grad = glu_grad * mask
    joined_grad = jnp.concatenate(
        [glu_grad * gate_sig, glu_grad * value * gate_sig * (1.0 - gate_sig)], axis=-1
    ).astype(jnp.bfloat16)
    lifted_grad = lax.dot_general(
        joined_grad, full_pointwise, (((1,), (1,)), ((), ())), preferred_element_type=jnp.float32
    )
    gain_term = jnp.sum(lifted_grad * normed, axis=0)
    grad_gain, grad_depthwise = lax.psum((gain_term, jnp.stack(tap_rows, axis=0)), ("seq", "fsdp"))
    scaled = lifted_grad * gain
    norm_grad = inverse * (
        scaled
        - jnp.mean(scaled, axis=-1, keepdims=True)
        - normed * jnp.mean(scaled * normed, axis=-1, keepdims=True)
    )
    grad_frames = (cotangent[0].astype(jnp.float32) + norm_grad).astype(jnp.bfloat16)
    term_pointwise = rounded_term(lifted, joined_grad)
    term_output = rounded_term(swished, branch_grad)
    owned = (
        lax.psum_scatter(
            term_pointwise.astype(jnp.bfloat16), "fsdp", scatter_dimension=0, tiled=True
        ).astype(jnp.float32),
        lax.psum_scatter(
            term_output.astype(jnp.bfloat16), "fsdp", scatter_dimension=0, tiled=True
        ).astype(jnp.float32),
    )
    grad_pointwise, grad_output = (
        lax.psum(owned[0].astype(jnp.bfloat16), "seq").astype(jnp.float32),
        lax.psum(owned[1].astype(jnp.bfloat16), "seq").astype(jnp.float32),
    )
    return (output[None], grad_frames[None], grad_pointwise, grad_output, grad_gain, grad_depthwise)


def solution(mesh):
    in_specs = (
        P("fsdp", "seq", None),
        P("fsdp"),
        P(),
        P("fsdp", None),
        P(),
        P("fsdp", None),
        P("fsdp", "seq", None),
    )
    out_specs = (
        P("fsdp", "seq", None),
        P("fsdp", "seq", None),
        P("fsdp", None),
        P("fsdp", None),
        P(),
        P(),
    )
    return jax.shard_map(
        on_device, mesh=mesh, in_specs=in_specs, out_specs=out_specs, check_vma=False
    )
```

profile of v0, /device:TPU:10, one launch (start us, length us, event | category | flops | bytes accessed | tf_op | source)
XLA Modules:
  0.0 515.2 jit_solution(6867970955985143212)
XLA Ops:
  9.4 1.7 convert_reduce_fusion
  12.0 87.0 %all-gather.3.cloned.1.call-done = bf16[1536,3072]{1,0:T(8,128)(2,1)} async-done(((bf16[192,3072]{1,0:T(8,128)(2,1)}), bf16[1536,3072]{1,0:T(8,128)(2,1)}) %all-gather.3.cloned.1.call-update) | async-done | bytes 9437200 | tf_op jit(solution)/shard_map/all_gather | solution.py:36
  99.1 7.7 %fusion.125 = f32[512,3072]{1,0:T(8,128)S(1)} fusion(bf16[1536,3072]{1,0:T(8,128)(2,1)} %all-gather.3.cloned.1.call-done, bf16[1,512,1536]{2,1,0:T(8,128)(2,1)S(1)} %copy-done.1, f32[1536]{0:T(1024)S(1)} %copy-done.41, f32[512]{0:T(512)S(1)} %add_rsqrt_fusion, f32[512]{0:T(512)S(1)} %broadcast_multiply_fusion.2), kind=kOutput, calls=%fused_computation.269 | convolution fusion | flops 4835770368 | bytes 17311744 | tf_op jit(solution)/shard_map/dot_general | solution.py:47
  107.6 1.8 copy-done
  109.5 3.4 collective-permute-start
  112.9 2.5 collective-permute-start.1
  115.6 4.1 collective-permute-done.1
  120.2 12.0 %multiply_add_fusion = f32[512,1536]{1,0:T(8,128)S(1)} fusion(f32[1,542,1536]{2,1,0:T(8,128)S(1)} %maximum_convert_fusion, f32[1536]{0:T(1024)S(1)} %get-tuple-element.69, f32[1536]{0:T(1024)S(1)} %get-tuple-element.70, f32[1536]{0:T(1024)S(1)} %get-tuple-element.41, f32[1536]{0:T(1024)S(1)} %get-tuple-element.42, f32[1536]{0:T(1024)S(1)} %get-tuple-element.43, ...), kind=kLoop, calls=%fused_computation.219 | loop fusion | flops 47972352 | bytes 100853760 | tf_op jit(solution)/shard_map/add | solution.py:54
  132.3 1.7 copy-done.4
  134.0 4.8 convolution_convert_fusion.1
  138.9 13.0 %all-gather.5.cloned.1.call-done = bf16[1536,1536]{1,0:T(8,128)(2,1)} async-done(((bf16[192,1536]{1,0:T(8,128)(2,1)}), bf16[1536,1536]{1,0:T(8,128)(2,1)}) %all-gather.5.cloned.1.call-update) | async-done | bytes 4718608 | tf_op jit(solution)/shard_map/all_gather | solution.py:37
  151.9 12.6 %fusion.46 = (f32[1536]{0:T(1024)}, f32[1536]{0:T(1024)}, f32[1536]{0:T(1024)}, f32[1536]{0:T(1024)}, f32[1536]{0:T(1024)}, /*index=5*/f32[1536]{0:T(1024)}, f32...) fusion(f32[1,542,1536]{2,1,0:T(8,128)S(1)} %maximum_convert_fus, ...), kind=kOutput, calls=%fused_computation.84 | convolution fusion | flops 2446569984 | bytes 51986432 | tf_op jit(solution)/shard_map/dot_general | solution.py:60
  165.4 3.4 collective-permute-start.2
  168.8 2.6 collective-permute-start.3
  171.5 4.2 collective-permute-done.3
  175.7 2.1 maximum_convert_fusion.1
  177.8 14.4 %multiply_convert_fusion.1 = (bf16[512,1536]{1,0:T(8,128)(2,1)S(1)}, f32[512,1536]{1,0:T(8,128)S(1)}) fusion(f32[512,3072]{1,0:T(8,128)} %copy-done, f32[512]{0:T(512)S(1)} %copy-done.25, f32[1,542,1536]{2,1,0:T(8,128)S(1)} %maximum_convert_fusion.1, f32[1536]{0:T(1024)S(1)} %copy-done.20, f32[1536]{0:T(1024)S(1)} %copy-done.22, ...), kind=kLoop, calls=%fused_computation.216 | loop fusion | flops 52690944 | bytes 105574400 | tf_op jit(solution)/shard_map/convert.1
  192.3 1.3 multiply_convert_fusion
  193.6 1.1 copy-done.7
  194.7 8.1 %convolution_convert_fusion = bf16[1536,3072]{1,0:T(8,128)(2,1)} fusion(bf16[512,1536]{1,0:T(8,128)(2,1)S(1)} %multiply_convert_fusion, bf16[512,1536]{1,0:T(8,128)(2,1)S(1)} %get-tuple-element.73, bf16[1,512,1536]{2,1,0:T(8,128)(2,1)S(1)} %copy-done.2, f32[1536]{0:T(1024)S(1)} %copy-done.42, f32[512]{0:T(512)S(1)} %copy-done.44, f32[512]{0:T(512)S(1)} %copy-done.27), kind=kOutput, calls=%fused_computation.31 | convolution fusion | flops 4846780416 | bytes 14166016 | tf_op jit(solution)/shard_map/dot_general | solution.py:23
  202.9 3.9 reduce-scatter.5.cloned.1.call-done
  206.7 100.1 %reduce-scatter.3.cloned.1.call-done = bf16[192,3072]{1,0:T(8,128)(2,1)} async-done(((bf16[1536,3072]{1,0:T(8,128)(2,1)}), bf16[192,3072]{1,0:T(8,128)(2,1)}) %reduce-scatter.3.cloned.1.call-update) | async-done | bytes 1179664 | tf_op jit(solution)/shard_map/reduce_scatter | solution.py:91
  307.2 8.3 %fusion.47 = (f32[1536]{0:T(1024)S(1)}, f32[1536]{0:T(1024)S(1)}, f32[1536]{0:T(1024)S(1)}, f32[1536]{0:T(1024)S(1)}, f32[1536]{0:T(1024)S(1)}, /*index=5*/f32[1...) fusion(bf16[512,1536]{1,0:T(8,128)(2,1)} %get-tuple-element.80,, ...), kind=kLoop, calls=%fused_computation.85 | loop fusion | flops 29070336 | bytes 58306560 | tf_op jit(solution)/shard_map/reduce_sum | solution.py:71
  316.1 2.8 stack.127
  318.9 7.7 %fusion.115 = bf16[1,512,1536]{2,1,0:T(8,128)(2,1)} fusion(bf16[1536,1536]{1,0:T(8,128)(2,1)} %all-gather.5.cloned.1.call-done, bf16[1,512,1536]{2,1,0:T(8,128)(2,1)} %param.7, f32[512,1536]{1,0:T(8,128)} %copy-done.4), kind=kOutput, calls=%fused_computation.224 | convolution fusion | flops 2422210560 | bytes 11010048 | tf_op jit(solution)/shard_map/dot_general | solution.py:57
  326.6 8.6 %fusion.13 = (f32[1536]{0:T(1024)S(1)}, f32[512]{0:T(512)S(1)}, f32[512]{0:T(512)S(1)}, f32[512,1536]{1,0:T(8,128)S(1)}) fusion(bf16[1,512,1536]{2,1,0:T(8,128)(2,1)S(1)} %copy-done.3, f32[512]{0:T(512)S(1)} %copy-done.44, f32[512]{0:T(512)S(1)} %copy-done.27, f32[1536]{0:T(1024)S(1)} %copy-done.42, bf16[1536,3072]{1,0:T(8,128)(2,1)} %all-gather.3.cloned.1.call-done, ...), kind=kOutput, calls=%fused_computation.51 | convolution fusion | flops 4845204992 | bytes 17321984 | tf_op jit(solution)/shard_map/dot_general | solution.py:76
  335.2 2.4 fusion.118
  337.7 43.1 %psum.30 = f32[1536]{0:T(1024)} all-reduce(f32[1536]{0:T(1024)S(1)} %get-tuple-element.37), channel_id=1, replica_groups=mesh['seq'=4,'fsdp'=8] {'seq','fsdp'}, use_global_device_ids=true, to_apply=%region_9.0 | all-reduce | flops 1536 | bytes 12288 | tf_op jit(solution)/shard_map/psum | solution.py:80
  380.7 3.0 convert_element_type.88
  383.7 1.1 convert_element_type.90
  384.9 121.9 %all-reduce.4.cloned.1.call-done = f32[31,1536]{1,0:T(8,128)} async-done(((f32[31,1536]{1,0:T(8,128)}), f32[31,1536]{1,0:T(8,128)}) %all-reduce.4.cloned.1.call-update) | async-done | bytes 190480 | tf_op jit(solution)/shard_map/psum | solution.py:80
  506.8 1.6 copy.17
  (149 shorter events, 5.6 us)
Async XLA Ops:
  7.2 91.9 %copy-start.41 = (f32[1536]{0:T(1024)S(1)}, f32[1536]{0:T(1024)}, u32[]{:S(2)}) copy-start(f32[1536]{0:T(1024)} %param.9) | copy-start | bytes 18436
  7.2 91.9 %all-gather.3.cloned.1.call-start = ((), (), s32[]{:S(2)}) async-start(), calls=%async_computation.2 | async-start | bytes 10616832 | tf_op jit(solution)/shard_map/all_gather | solution.py:36
  7.9 144.0 %all-gather.5.cloned.1.call-start = ((), (), s32[]{:S(2)}) async-start(), calls=%async_computation.3 | async-start | bytes 5308416 | tf_op jit(solution)/shard_map/all_gather | solution.py:37
  8.7 198.1 %reduce-scatter.5.cloned.1.call-start = ((), (), s32[]{:S(2)}) async-start(), calls=%async_computation.5 | async-start | bytes 5308416 | tf_op jit(solution)/shard_map/reduce_scatter | solution.py:94
  11.1 95.6 %copy-start.26 = (f32[512]{0:T(512)}, f32[512]{0:T(512)S(1)}, u32[]{:S(2)}) copy-start(f32[512]{0:T(512)S(1)} %broadcast_multiply_fusion.2) | copy-start | bytes 6148
  11.7 95.1 %copy-start.43 = (f32[512]{0:T(512)}, f32[512]{0:T(512)S(1)}, u32[]{:S(2)}) copy-start(f32[512]{0:T(512)S(1)} %add_rsqrt_fusion) | copy-start | bytes 6148
  12.0 94.7 %copy-start.23 = (f32[512]{0:T(512)}, f32[512]{0:T(512)S(1)}, u32[]{:S(2)}) copy-start(f32[512]{0:T(512)S(1)} %fusion.121) | copy-start | bytes 6148
  109.5 6.1 %collective-permute-start = (bf16[1,15,1536]{2,1,0:T(8,128)(2,1)S(1)}, bf16[1,15,1536]{2,1,0:T(8,128)(2,1)S(1)}, u32[]{:S(2)}, u32[]{:S(2)}) collective-permute-start(bf16[1,15,1536]{2,1,0:T(8,128)(2,1)S(1)} %get-tuple-element.77), channel_id=1, source_target_pairs={{0,8},{8,16},{16,24},{1,9},{9,17},{17,25},{2,10},{10,18},{18,26},{... | collective-permute-start | bytes 138248 | tf_op jit(solution)/shard_map/ppermute | solution.py:14
  112.9 6.9 %collective-permute-start.1 = (bf16[1,15,1536]{2,1,0:T(8,128)(2,1)S(1)}, bf16[1,15,1536]{2,1,0:T(8,128)(2,1)S(1)}, u32[]{:S(2)}, u32[]{:S(2)}) collective-permute-start(bf16[1,15,1536]{2,1,0:T(8,128)(2,1)S(1)} %get-tuple-element.78), channel_id=1, source_target_pairs={{8,0},{16,8},{24,16},{9,1},{17,9},{25,17},{10,2},{18,10},{26,18},{... | collective-permute-start | bytes 138248 | tf_op jit(solution)/shard_map/ppermute | solution.py:17
  115.5 16.7 %copy-start.13 = (f32[1536]{0:T(1024)}, f32[1536]{0:T(1024)S(1)}, u32[]{:S(2)}) copy-start(f32[1536]{0:T(1024)S(1)} %get-tuple-element.66) | copy-start | bytes 18436
  115.5 16.7 %copy-start.15 = (f32[1536]{0:T(1024)}, f32[1536]{0:T(1024)S(1)}, u32[]{:S(2)}) copy-start(f32[1536]{0:T(1024)S(1)} %get-tuple-element.67) | copy-start | bytes 18436
  115.5 16.7 %copy-start.17 = (f32[1536]{0:T(1024)}, f32[1536]{0:T(1024)S(1)}, u32[]{:S(2)}) copy-start(f32[1536]{0:T(1024)S(1)} %get-tuple-element.68) | copy-start | bytes 18436
  115.6 16.7 %copy-start.19 = (f32[1536]{0:T(1024)}, f32[1536]{0:T(1024)S(1)}, u32[]{:S(2)}) copy-start(f32[1536]{0:T(1024)S(1)} %get-tuple-element.69) | copy-start | bytes 18436
  115.6 16.7 %copy-start.21 = (f32[1536]{0:T(1024)}, f32[1536]{0:T(1024)S(1)}, u32[]{:S(2)}) copy-start(f32[1536]{0:T(1024)S(1)} %get-tuple-element.70) | copy-start | bytes 18436
  120.2 13.8 %copy-start.5 = (bf16[1,512,1536]{2,1,0:T(8,128)(2,1)S(1)}, bf16[1,512,1536]{2,1,0:T(8,128)(2,1)}, u32[]{:S(2)}) copy-start(bf16[1,512,1536]{2,1,0:T(8,128)(2,1)} %param.13) | copy-start | bytes 4718596
  120.2 13.8 %copy-start.24 = (f32[512]{0:T(512)S(1)}, f32[512]{0:T(512)}, u32[]{:S(2)}) copy-start(f32[512]{0:T(512)} %copy-done.23) | copy-start | bytes 6148
  138.9 167.9 %reduce-scatter.3.cloned.1.call-start = ((), (), s32[]{:S(2)}) async-start(), calls=%async_computation.4 | async-start | bytes 10616832 | tf_op jit(solution)/shard_map/reduce_scatter | solution.py:91
  164.5 13.3 %copy-start.14 = (f32[1536]{0:T(1024)S(1)}, f32[1536]{0:T(1024)}, u32[]{:S(2)}) copy-start(f32[1536]{0:T(1024)} %copy-done.13) | copy-start | bytes 18436
  164.5 13.3 %copy-start.16 = (f32[1536]{0:T(1024)S(1)}, f32[1536]{0:T(1024)}, u32[]{:S(2)}) copy-start(f32[1536]{0:T(1024)} %copy-done.15) | copy-start | bytes 18436
  164.5 13.3 %copy-start.18 = (f32[1536]{0:T(1024)S(1)}, f32[1536]{0:T(1024)}, u32[]{:S(2)}) copy-start(f32[1536]{0:T(1024)} %copy-done.17) | copy-start | bytes 18436
  164.5 13.3 %copy-start.20 = (f32[1536]{0:T(1024)S(1)}, f32[1536]{0:T(1024)}, u32[]{:S(2)}) copy-start(f32[1536]{0:T(1024)} %copy-done.19) | copy-start | bytes 18436
  164.5 13.3 %copy-start.22 = (f32[1536]{0:T(1024)S(1)}, f32[1536]{0:T(1024)}, u32[]{:S(2)}) copy-start(f32[1536]{0:T(1024)} %copy-done.21) | copy-start | bytes 18436
  164.5 13.3 %copy-start.25 = (f32[512]{0:T(512)S(1)}, f32[512]{0:T(512)}, u32[]{:S(2)}) copy-start(f32[512]{0:T(512)} %copy-done.23) | copy-start | bytes 6148
  165.4 6.0 %collective-permute-start.2 = (bf16[1,15,1536]{2,1,0:T(8,128)(2,1)S(1)}, bf16[1,15,1536]{2,1,0:T(8,128)(2,1)S(1)}, u32[]{:S(2)}, u32[]{:S(2)}) collective-permute-start(bf16[1,15,1536]{2,1,0:T(8,128)(2,1)S(1)} %get-tuple-element.75), channel_id=1, source_target_pairs={{0,8},{8,16},{16,24},{1,9},{9,17},{17,25},{2,10},{10,18},{18,26},{... | collective-permute-start | bytes 138248 | tf_op jit(solution)/shard_map/ppermute | solution.py:14
  168.8 6.9 %collective-permute-start.3 = (bf16[1,15,1536]{2,1,0:T(8,128)(2,1)S(1)}, bf16[1,15,1536]{2,1,0:T(8,128)(2,1)S(1)}, u32[]{:S(2)}, u32[]{:S(2)}) collective-permute-start(bf16[1,15,1536]{2,1,0:T(8,128)(2,1)S(1)} %get-tuple-element.76), channel_id=1, source_target_pairs={{8,0},{16,8},{24,16},{9,1},{17,9},{25,17},{10,2},{18,10},{26,18},{... | collective-permute-start | bytes 138248 | tf_op jit(solution)/shard_map/ppermute | solution.py:17
  175.7 16.5 %slice-start = ((s8[6291456]{0:T(1024)(128)(4,1)}), s8[4194304]{0:T(1024)(128)(4,1)S(1)}, s32[]{:S(2)}) async-start(s8[6291456]{0:T(1024)(128)(4,1)} %bitcast.526), calls=%async_computation.8 | async-start | bytes 8388608
  177.8 14.4 %slice-start.1 = ((s8[6291456]{0:T(1024)(128)(4,1)}), s8[2097152]{0:T(1024)(128)(4,1)S(1)}, s32[]{:S(2)}) async-start(s8[6291456]{0:T(1024)(128)(4,1)} %bitcast.526), calls=%async_computation.9 | async-start | bytes 4194304
  202.8 177.9 %all-reduce.6.cloned.1.call-start = ((), (), s32[]{:S(2)}) async-start(), calls=%async_computation.7 | async-start | bytes 3538944 | tf_op jit(solution)/shard_map/psum | solution.py:99
  306.9 8.9 %copy-start.30 = (f32[1536]{0:T(1024)S(1)}, f32[1536]{0:T(1024)}, u32[]{:S(2)}) copy-start(f32[1536]{0:T(1024)} %get-tuple-element.34) | copy-start | bytes 18436
  306.9 8.9 %copy-start.29 = (f32[1536]{0:T(1024)S(1)}, f32[1536]{0:T(1024)}, u32[]{:S(2)}) copy-start(f32[1536]{0:T(1024)} %get-tuple-element.35) | copy-start | bytes 18436
  307.0 8.9 %copy-start.28 = (f32[1536]{0:T(1024)S(1)}, f32[1536]{0:T(1024)}, u32[]{:S(2)}) copy-start(f32[1536]{0:T(1024)} %get-tuple-element.36) | copy-start | bytes 18436
  307.0 199.8 %all-reduce.4.cloned.1.call-start = ((), (), s32[]{:S(2)}) async-start(), calls=%async_computation.6 | async-start | bytes 393216 | tf_op jit(solution)/shard_map/psum | solution.py:80
  (25 other events, 147.9 us)
Sparse Core Ops, SparseCore 0:
  9.7 89.3 all-gather.2
  100.7 51.1 all-gather.4
  154.2 52.4 reduce-scatter.4
  208.9 97.8 reduce-scatter.2
  309.9 65.7 all-reduce.5
  381.6 125.0 all-reduce.3
where the time goes:
time: 516 us; the launch traced here: 515 us
  waiting for transfers between devices  336 us (65%)
  matrix products  49.4 us (10%)
  other arithmetic  48.1 us (9%)
  blocking collectives  43.1 us (8%)
  between operations  15.8 us (3%)
  starting transfers between devices  12.3 us (2%)
  local copies, waits for them, and re-layouts  10.9 us (2%)
    psum x1, waiting for transfers between devices, on_device(): lax.psum((gain_term, jnp.stack(tap_rows, axis=0)), ('seq', 'fsdp'))  122 us
    reduce_scatter x1, waiting for transfers between devices, on_device(): lax.psum_scatter(term_pointwise.astype(jnp.bfloat16), 'fsdp', scatter_dim...  100 us
    all_gather x1, waiting for transfers between devices, on_device(): lax.all_gather(w_pointwise, 'fsdp', axis=0, tiled=True)  87 us
    psum x1, blocking collectives, on_device(): lax.psum((gain_term, jnp.stack(tap_rows, axis=0)), ('seq', 'fsdp'))  43.1 us
    another operation x2, other arithmetic  15.6 us
    all_gather x1, waiting for transfers between devices, on_device(): lax.all_gather(w_output, 'fsdp', axis=0, tiled=True)  13 us
    dot_general x2, matrix products, rounded_term(): lax.dot_general(left, right, (((0,), (0,)), ((), ())), preferred_element_...  12.9 us
    dot_general x1, matrix products, on_device(): lax.dot_general(branch_grad, full_output, (((1,), (1,)), ((), ())), prefe...  12.6 us
  transfers between devices with their start and end apart: 10, of which 7 were waited for; matrix products, arithmetic and copies ran while one was open for 20% of the time, Pallas kernels for 0%

commit v1 on v0

--- a/solution.py
+++ b/solution.py
@@ -1,9 +1,19 @@
+import functools
 import jax
 import jax.numpy as jnp
 from jax import lax
 from jax.sharding import PartitionSpec as P
 
 EPS = 1e-05
+
+
+def _answer_series(obj, named_axis, dev_axis):
+    kept_arr = jax.lax.psum(obj, named_axis)
+    earlier = jax.lax.psum(kept_arr, dev_axis)
+    return earlier
+
+
+work_chains = functools.partial(_answer_series, named_axis="fsdp", dev_axis="seq")
 
 
 def extended(block, sides, width):
@@ -77,7 +87,7 @@
         joined_grad, full_pointwise, (((1,), (1,)), ((), ())), preferred_element_type=jnp.float32
     )
     gain_term = jnp.sum(lifted_grad * normed, axis=0)
-    grad_gain, grad_depthwise = lax.psum((gain_term, jnp.stack(tap_rows, axis=0)), ("seq", "fsdp"))
+    grad_gain, grad_depthwise = work_chains((gain_term, jnp.stack(tap_rows, axis=0)))
     scaled = lifted_grad * gain
     norm_grad = inverse * (
         scaled

time: 516 us -> 488 us (0.946)
  blocking collectives: 43.1 us -> 20.1 us
  waiting for transfers between devices: 336 us -> 325 us
    psum x1, waiting for transfers between devices: 0.01 us -> 43.6 us  [on_device(): lax.psum(owned[0].astype(jnp.bfloat16), 'seq').astype(jnp.float32)]
    psum x1 -> x2, waiting for transfers between devices: 122 us -> 80 us  [the longest x1 41.5 us: _answer_series(): earlier = jax.lax.psum(kept_arr, dev_axis)]
    psum x1 -> x2, blocking collectives: 43.1 us -> 20.1 us  [the longest x1 11.3 us: _answer_series(): kept_arr = jax.lax.psum(obj, named_axis)]
    reduce_scatter x1, waiting for transfers between devices: 100 us -> 92 us  [on_device(): lax.psum_scatter(term_pointwise.astype(jnp.bfloat16), 'fsdp', scatter_dim...]
  transfers between devices with their start and end apart: 10 -> 11, of which waited for: 7 -> 8; matrix products, arithmetic and copies ran while one was open for 20% -> 22% of each run, Pallas kernels for 0% -> 0%
where the time goes in v1:
time: 488 us; the launch traced here: 486 us
  waiting for transfers between devices  325 us (67%)
  matrix products  51.9 us (11%)
  other arithmetic  50 us (10%)
  blocking collectives  20.1 us (4%)
  between operations  15.8 us (3%)
  starting transfers between devices  12.4 us (3%)
  local copies, waits for them, and re-layouts  10.9 us (2%)
    reduce_scatter x1, waiting for transfers between devices, on_device(): lax.psum_scatter(term_pointwise.astype(jnp.bfloat16), 'fsdp', scatter_dim...  92 us
    all_gather x1, waiting for transfers between devices, on_device(): lax.all_gather(w_pointwise, 'fsdp', axis=0, tiled=True)  87 us
    psum x1, waiting for transfers between devices, on_device(): lax.psum(owned[0].astype(jnp.bfloat16), 'seq').astype(jnp.float32)  43.6 us
    psum x1, waiting for transfers between devices, _answer_series(): earlier = jax.lax.psum(kept_arr, dev_axis)  41.5 us
    psum x1, waiting for transfers between devices, _answer_series(): kept_arr = jax.lax.psum(obj, named_axis)  38.5 us
    another operation x2, other arithmetic  15.6 us
    all_gather x1, waiting for transfers between devices, on_device(): lax.all_gather(w_output, 'fsdp', axis=0, tiled=True)  13 us
    dot_general x2, matrix products, rounded_term(): lax.dot_general(left, right, (((0,), (0,)), ((), ())), preferred_element_...  12.9 us
  transfers between devices with their start and end apart: 11, of which 8 were waited for; matrix products, arithmetic and copies ran while one was open for 22% of the time, Pallas kernels for 0%

profile of v1, /device:TPU:10, one launch (start us, length us, event | category | flops | bytes accessed | tf_op | source)
XLA Modules:
  0.0 486.5 jit_solution(10289992672641010439)
XLA Ops:
  9.4 1.7 convert_reduce_fusion
  12.0 87.0 %all-gather.3.cloned.1.call-done = bf16[1536,3072]{1,0:T(8,128)(2,1)} async-done(((bf16[192,3072]{1,0:T(8,128)(2,1)}), bf16[1536,3072]{1,0:T(8,128)(2,1)}) %all-gather.3.cloned.1.call-update) | async-done | bytes 9437200 | tf_op jit(solution)/shard_map/all_gather | solution.py:46
  99.1 7.7 %fusion.125 = f32[512,3072]{1,0:T(8,128)S(1)} fusion(bf16[1536,3072]{1,0:T(8,128)(2,1)} %all-gather.3.cloned.1.call-done, bf16[1,512,1536]{2,1,0:T(8,128)(2,1)S(1)} %copy-done.1, f32[1536]{0:T(1024)S(1)} %copy-done.41, f32[512]{0:T(512)S(1)} %add_rsqrt_fusion, f32[512]{0:T(512)S(1)} %broadcast_multiply_fusion.2), kind=kOutput, calls=%fused_computation.269 | convolution fusion | flops 4835770368 | bytes 17311744 | tf_op jit(solution)/shard_map/dot_general | solution.py:57
  107.6 1.8 copy-done
  109.5 3.4 collective-permute-start
  112.9 2.5 collective-permute-start.1
  115.6 4.1 collective-permute-done.1
  120.2 12.0 %multiply_add_fusion = f32[512,1536]{1,0:T(8,128)S(1)} fusion(f32[1,542,1536]{2,1,0:T(8,128)S(1)} %maximum_convert_fusion, f32[1536]{0:T(1024)S(1)} %get-tuple-element.69, f32[1536]{0:T(1024)S(1)} %get-tuple-element.70, f32[1536]{0:T(1024)S(1)} %get-tuple-element.41, f32[1536]{0:T(1024)S(1)} %get-tuple-element.42, f32[1536]{0:T(1024)S(1)} %get-tuple-element.43, ...), kind=kLoop, calls=%fused_computation.219 | loop fusion | flops 47972352 | bytes 100853760 | tf_op jit(solution)/shard_map/add | solution.py:64
  132.3 1.7 copy-done.4
  134.0 4.8 convolution_convert_fusion.1
  138.9 13.0 %all-gather.5.cloned.1.call-done = bf16[1536,1536]{1,0:T(8,128)(2,1)} async-done(((bf16[192,1536]{1,0:T(8,128)(2,1)}), bf16[1536,1536]{1,0:T(8,128)(2,1)}) %all-gather.5.cloned.1.call-update) | async-done | bytes 4718608 | tf_op jit(solution)/shard_map/all_gather | solution.py:47
  151.9 12.6 %fusion.46 = (f32[1536]{0:T(1024)}, f32[1536]{0:T(1024)}, f32[1536]{0:T(1024)}, f32[1536]{0:T(1024)}, f32[1536]{0:T(1024)}, /*index=5*/f32[1536]{0:T(1024)}, f32...) fusion(f32[1,542,1536]{2,1,0:T(8,128)S(1)} %maximum_convert_fus, ...), kind=kOutput, calls=%fused_computation.84 | convolution fusion | flops 2446569984 | bytes 51986432 | tf_op jit(solution)/shard_map/dot_general | solution.py:70
  165.4 3.4 collective-permute-start.2
  168.8 2.6 collective-permute-start.3
  171.5 4.2 collective-permute-done.3
  175.7 2.1 maximum_convert_fusion.1
  177.8 14.4 %multiply_convert_fusion.1 = (bf16[512,1536]{1,0:T(8,128)(2,1)S(1)}, f32[512,1536]{1,0:T(8,128)S(1)}) fusion(f32[512,3072]{1,0:T(8,128)} %copy-done, f32[512]{0:T(512)S(1)} %copy-done.25, f32[1,542,1536]{2,1,0:T(8,128)S(1)} %maximum_convert_fusion.1, f32[1536]{0:T(1024)S(1)} %copy-done.20, f32[1536]{0:T(1024)S(1)} %copy-done.22, ...), kind=kLoop, calls=%fused_computation.216 | loop fusion | flops 52690944 | bytes 105574400 | tf_op jit(solution)/shard_map/convert.1
  192.3 1.3 multiply_convert_fusion
  194.7 8.1 %convolution_convert_fusion = bf16[1536,3072]{1,0:T(8,128)(2,1)} fusion(bf16[512,1536]{1,0:T(8,128)(2,1)S(1)} %multiply_convert_fusion, bf16[512,1536]{1,0:T(8,128)(2,1)S(1)} %get-tuple-element.73, bf16[1,512,1536]{2,1,0:T(8,128)(2,1)S(1)} %copy-done.2, f32[1536]{0:T(1024)S(1)} %copy-done.42, f32[512]{0:T(512)S(1)} %copy-done.44, f32[512]{0:T(512)S(1)} %copy-done.27), kind=kOutput, calls=%fused_computation.31 | convolution fusion | flops 4846780416 | bytes 14166016 | tf_op jit(solution)/shard_map/dot_general | solution.py:33
  203.0 8.3 %fusion.47 = (f32[1536]{0:T(1024)S(1)}, f32[1536]{0:T(1024)S(1)}, f32[1536]{0:T(1024)S(1)}, f32[1536]{0:T(1024)S(1)}, f32[1536]{0:T(1024)S(1)}, /*index=5*/f32[1...) fusion(bf16[512,1536]{1,0:T(8,128)(2,1)} %get-tuple-element.80,, ...), kind=kLoop, calls=%fused_computation.85 | loop fusion | flops 29070336 | bytes 58306560 | tf_op jit(solution)/shard_map/reduce_sum | solution.py:81
  211.9 2.8 stack.127
  214.8 92.0 %reduce-scatter.3.cloned.1.call-done = bf16[192,3072]{1,0:T(8,128)(2,1)} async-done(((bf16[1536,3072]{1,0:T(8,128)(2,1)}), bf16[192,3072]{1,0:T(8,128)(2,1)}) %reduce-scatter.3.cloned.1.call-update) | async-done | bytes 1179664 | tf_op jit(solution)/shard_map/reduce_scatter | solution.py:101
  307.1 7.6 %fusion.115 = bf16[1,512,1536]{2,1,0:T(8,128)(2,1)} fusion(bf16[1536,1536]{1,0:T(8,128)(2,1)} %all-gather.5.cloned.1.call-done, bf16[1,512,1536]{2,1,0:T(8,128)(2,1)} %param.7, f32[512,1536]{1,0:T(8,128)} %copy-done.4), kind=kOutput, calls=%fused_computation.224 | convolution fusion | flops 2422210560 | bytes 11010048 | tf_op jit(solution)/shard_map/dot_general | solution.py:67
  314.8 11.1 %fusion.13 = (f32[1536]{0:T(1024)S(1)}, f32[512]{0:T(512)S(1)}, f32[512]{0:T(512)S(1)}, f32[512,1536]{1,0:T(8,128)}) fusion(bf16[1,512,1536]{2,1,0:T(8,128)(2,1)S(1)} %copy-done.3, f32[512]{0:T(512)S(1)} %copy-done.44, f32[512]{0:T(512)S(1)} %copy-done.27, f32[1536]{0:T(1024)S(1)} %copy-done.42, bf16[1536,3072]{1,0:T(8,128)(2,1)} %all-gather.3.cloned.1.call-done, ...), kind=kOutput, calls=%fused_computation.51 | convolution fusion | flops 4845204992 | bytes 17321984 | tf_op jit(solution)/shard_map/dot_general | solution.py:86
  325.9 38.5 %all-reduce.5.cloned.1.call-done = f32[31,1536]{1,0:T(8,128)} async-done(((f32[31,1536]{1,0:T(8,128)}), f32[31,1536]{1,0:T(8,128)}) %all-reduce.5.cloned.1.call-update) | async-done | bytes 190480 | tf_op jit(solution)/shard_map/psum | solution.py:11
  364.4 4.3 fusion.118
  368.7 11.3 %psum.44 = f32[1536]{0:T(1024)S(1)} all-reduce(f32[1536]{0:T(1024)S(1)} %get-tuple-element.37), channel_id=1, replica_groups=mesh['seq'=4,'fsdp'=8] {'fsdp'}, use_global_device_ids=true, to_apply=%region_9.0 | all-reduce | flops 1536 | bytes 12288 | tf_op jit(solution)/shard_map/psum | solution.py:11
  380.0 8.8 %psum.45 = f32[1536]{0:T(1024)} all-reduce(f32[1536]{0:T(1024)S(1)} %psum.44), channel_id=1, replica_groups=mesh['seq'=4,'fsdp'=8] {'seq'}, use_global_device_ids=true, to_apply=%region_10.0 | all-reduce | flops 1536 | bytes 12288 | tf_op jit(solution)/shard_map/psum | solution.py:12
  388.8 43.6 %all-reduce.9.cloned.1.call-done = (bf16[192,3072]{1,0:T(8,128)(2,1)}, bf16[192,1536]{1,0:T(8,128)(2,1)}) async-done(((bf16[192,3072]{1,0:T(8,128)(2,1)}, bf16[192,1536]{1,0:T(8,128)(2,1)}), (bf16[192,3072]{1,0:T(8,128)(2,1)}, bf16[192,1536]{1,0:T(8,128)(2,1)})) %all-reduce.9.cloned.1.call-update) | async-done | bytes 1769488 | tf_op jit(solution)/shard_map/psum | solution.py:109
  432.4 3.0 convert_element_type.88
  436.5 41.5 %all-reduce.7.cloned.1.call-done = f32[31,1536]{1,0:T(8,128)} async-done(((f32[31,1536]{1,0:T(8,128)}), f32[31,1536]{1,0:T(8,128)}) %all-reduce.7.cloned.1.call-update) | async-done | bytes 190480 | tf_op jit(solution)/shard_map/psum | solution.py:12
  478.0 1.6 copy.18
  (153 shorter events, 8.0 us)
Async XLA Ops:
  7.2 91.9 %copy-start.41 = (f32[1536]{0:T(1024)S(1)}, f32[1536]{0:T(1024)}, u32[]{:S(2)}) copy-start(f32[1536]{0:T(1024)} %param.9) | copy-start | bytes 18436
  7.2 91.9 %all-gather.3.cloned.1.call-start = ((), (), s32[]{:S(2)}) async-start(), calls=%async_computation.2 | async-start | bytes 10616832 | tf_op jit(solution)/shard_map/all_gather | solution.py:46
  7.9 144.0 %all-gather.5.cloned.1.call-start = ((), (), s32[]{:S(2)}) async-start(), calls=%async_computation.3 | async-start | bytes 5308416 | tf_op jit(solution)/shard_map/all_gather | solution.py:47
  8.7 206.1 %reduce-scatter.5.cloned.1.call-start = ((), (), s32[]{:S(2)}) async-start(), calls=%async_computation.5 | async-start | bytes 5308416 | tf_op jit(solution)/shard_map/reduce_scatter | solution.py:104
  11.1 95.6 %copy-start.26 = (f32[512]{0:T(512)}, f32[512]{0:T(512)S(1)}, u32[]{:S(2)}) copy-start(f32[512]{0:T(512)S(1)} %broadcast_multiply_fusion.2) | copy-start | bytes 6148
  11.7 95.1 %copy-start.43 = (f32[512]{0:T(512)}, f32[512]{0:T(512)S(1)}, u32[]{:S(2)}) copy-start(f32[512]{0:T(512)S(1)} %add_rsqrt_fusion) | copy-start | bytes 6148
  12.0 94.7 %copy-start.23 = (f32[512]{0:T(512)}, f32[512]{0:T(512)S(1)}, u32[]{:S(2)}) copy-start(f32[512]{0:T(512)S(1)} %fusion.121) | copy-start | bytes 6148
  109.5 6.1 %collective-permute-start = (bf16[1,15,1536]{2,1,0:T(8,128)(2,1)S(1)}, bf16[1,15,1536]{2,1,0:T(8,128)(2,1)S(1)}, u32[]{:S(2)}, u32[]{:S(2)}) collective-permute-start(bf16[1,15,1536]{2,1,0:T(8,128)(2,1)S(1)} %get-tuple-element.77), channel_id=1, source_target_pairs={{0,8},{8,16},{16,24},{1,9},{9,17},{17,25},{2,10},{10,18},{18,26},{... | collective-permute-start | bytes 138248 | tf_op jit(solution)/shard_map/ppermute | solution.py:24
  112.9 6.9 %collective-permute-start.1 = (bf16[1,15,1536]{2,1,0:T(8,128)(2,1)S(1)}, bf16[1,15,1536]{2,1,0:T(8,128)(2,1)S(1)}, u32[]{:S(2)}, u32[]{:S(2)}) collective-permute-start(bf16[1,15,1536]{2,1,0:T(8,128)(2,1)S(1)} %get-tuple-element.78), channel_id=1, source_target_pairs={{8,0},{16,8},{24,16},{9,1},{17,9},{25,17},{10,2},{18,10},{26,18},{... | collective-permute-start | bytes 138248 | tf_op jit(solution)/shard_map/ppermute | solution.py:27
  115.5 16.7 %copy-start.13 = (f32[1536]{0:T(1024)}, f32[1536]{0:T(1024)S(1)}, u32[]{:S(2)}) copy-start(f32[1536]{0:T(1024)S(1)} %get-tuple-element.66) | copy-start | bytes 18436
  115.5 16.7 %copy-start.15 = (f32[1536]{0:T(1024)}, f32[1536]{0:T(1024)S(1)}, u32[]{:S(2)}) copy-start(f32[1536]{0:T(1024)S(1)} %get-tuple-element.67) | copy-start | bytes 18436
  115.5 16.7 %copy-start.17 = (f32[1536]{0:T(1024)}, f32[1536]{0:T(1024)S(1)}, u32[]{:S(2)}) copy-start(f32[1536]{0:T(1024)S(1)} %get-tuple-element.68) | copy-start | bytes 18436
  115.6 16.7 %copy-start.19 = (f32[1536]{0:T(1024)}, f32[1536]{0:T(1024)S(1)}, u32[]{:S(2)}) copy-start(f32[1536]{0:T(1024)S(1)} %get-tuple-element.69) | copy-start | bytes 18436
  115.6 16.7 %copy-start.21 = (f32[1536]{0:T(1024)}, f32[1536]{0:T(1024)S(1)}, u32[]{:S(2)}) copy-start(f32[1536]{0:T(1024)S(1)} %get-tuple-element.70) | copy-start | bytes 18436
  120.2 13.8 %copy-start.5 = (bf16[1,512,1536]{2,1,0:T(8,128)(2,1)S(1)}, bf16[1,512,1536]{2,1,0:T(8,128)(2,1)}, u32[]{:S(2)}) copy-start(bf16[1,512,1536]{2,1,0:T(8,128)(2,1)} %param.13) | copy-start | bytes 4718596
  120.2 13.8 %copy-start.24 = (f32[512]{0:T(512)S(1)}, f32[512]{0:T(512)}, u32[]{:S(2)}) copy-start(f32[512]{0:T(512)} %copy-done.23) | copy-start | bytes 6148
  138.9 167.9 %reduce-scatter.3.cloned.1.call-start = ((), (), s32[]{:S(2)}) async-start(), calls=%async_computation.4 | async-start | bytes 10616832 | tf_op jit(solution)/shard_map/reduce_scatter | solution.py:101
  164.5 13.3 %copy-start.14 = (f32[1536]{0:T(1024)S(1)}, f32[1536]{0:T(1024)}, u32[]{:S(2)}) copy-start(f32[1536]{0:T(1024)} %copy-done.13) | copy-start | bytes 18436
  164.5 13.3 %copy-start.16 = (f32[1536]{0:T(1024)S(1)}, f32[1536]{0:T(1024)}, u32[]{:S(2)}) copy-start(f32[1536]{0:T(1024)} %copy-done.15) | copy-start | bytes 18436
  164.5 13.3 %copy-start.18 = (f32[1536]{0:T(1024)S(1)}, f32[1536]{0:T(1024)}, u32[]{:S(2)}) copy-start(f32[1536]{0:T(1024)} %copy-done.17) | copy-start | bytes 18436
  164.5 13.3 %copy-start.20 = (f32[1536]{0:T(1024)S(1)}, f32[1536]{0:T(1024)}, u32[]{:S(2)}) copy-start(f32[1536]{0:T(1024)} %copy-done.19) | copy-start | bytes 18436
  164.5 13.3 %copy-start.22 = (f32[1536]{0:T(1024)S(1)}, f32[1536]{0:T(1024)}, u32[]{:S(2)}) copy-start(f32[1536]{0:T(1024)} %copy-done.21) | copy-start | bytes 18436
  164.5 13.3 %copy-start.25 = (f32[512]{0:T(512)S(1)}, f32[512]{0:T(512)}, u32[]{:S(2)}) copy-start(f32[512]{0:T(512)} %copy-done.23) | copy-start | bytes 6148
  165.4 6.0 %collective-permute-start.2 = (bf16[1,15,1536]{2,1,0:T(8,128)(2,1)S(1)}, bf16[1,15,1536]{2,1,0:T(8,128)(2,1)S(1)}, u32[]{:S(2)}, u32[]{:S(2)}) collective-permute-start(bf16[1,15,1536]{2,1,0:T(8,128)(2,1)S(1)} %get-tuple-element.75), channel_id=1, source_target_pairs={{0,8},{8,16},{16,24},{1,9},{9,17},{17,25},{2,10},{10,18},{18,26},{... | collective-permute-start | bytes 138248 | tf_op jit(solution)/shard_map/ppermute | solution.py:24
  168.8 6.9 %collective-permute-start.3 = (bf16[1,15,1536]{2,1,0:T(8,128)(2,1)S(1)}, bf16[1,15,1536]{2,1,0:T(8,128)(2,1)S(1)}, u32[]{:S(2)}, u32[]{:S(2)}) collective-permute-start(bf16[1,15,1536]{2,1,0:T(8,128)(2,1)S(1)} %get-tuple-element.76), channel_id=1, source_target_pairs={{8,0},{16,8},{24,16},{9,1},{17,9},{25,17},{10,2},{18,10},{26,18},{... | collective-permute-start | bytes 138248 | tf_op jit(solution)/shard_map/ppermute | solution.py:27
  175.7 16.5 %slice-start = ((s8[6291456]{0:T(1024)(128)(4,1)}), s8[4194304]{0:T(1024)(128)(4,1)S(1)}, s32[]{:S(2)}) async-start(s8[6291456]{0:T(1024)(128)(4,1)} %bitcast.526), calls=%async_computation.9 | async-start | bytes 8388608
  177.8 14.4 %slice-start.1 = ((s8[6291456]{0:T(1024)(128)(4,1)}), s8[2097152]{0:T(1024)(128)(4,1)S(1)}, s32[]{:S(2)}) async-start(s8[6291456]{0:T(1024)(128)(4,1)} %bitcast.526), calls=%async_computation.10 | async-start | bytes 4194304
  202.9 8.7 %copy-start.28 = (f32[1536]{0:T(1024)S(1)}, f32[1536]{0:T(1024)}, u32[]{:S(2)}) copy-start(f32[1536]{0:T(1024)} %get-tuple-element.36) | copy-start | bytes 18436
  203.0 161.4 %all-reduce.5.cloned.1.call-start = ((), (), s32[]{:S(2)}) async-start(), calls=%async_computation.6 | async-start | bytes 393216 | tf_op jit(solution)/shard_map/psum | solution.py:11
  214.7 217.7 %all-reduce.9.cloned.1.call-start = ((), (), s32[]{:S(2)}) async-start(), calls=%async_computation.8 | async-start | bytes 3538944 | tf_op jit(solution)/shard_map/psum | solution.py:109
  306.8 171.2 %all-reduce.7.cloned.1.call-start = ((), (), s32[]{:S(2)}) async-start(), calls=%async_computation.7 | async-start | bytes 393216 | tf_op jit(solution)/shard_map/psum | solution.py:12
  314.8 49.6 %copy-start.6 = (bf16[1,512,1536]{2,1,0:T(8,128)(2,1)S(1)}, bf16[1,512,1536]{2,1,0:T(8,128)(2,1)}, u32[]{:S(2)}) copy-start(bf16[1,512,1536]{2,1,0:T(8,128)(2,1)} %param.13) | copy-start | bytes 4718596
  (26 other events, 154.8 us)
Sparse Core Ops, SparseCore 0:
  9.7 89.3 all-gather.2
  100.7 51.1 all-gather.4
  154.2 52.4 reduce-scatter.4
  208.9 97.8 reduce-scatter.2
  309.5 54.7 all-reduce.4
  367.8 64.5 all-reduce.8
  435.5 42.4 all-reduce.6
